TPU v7x, 32 devices: a whole 2x2x4 slice. The times are simulated.
32 devices in a mesh: stn: 8 (over z, x), tm: 4 (over y, core).
Axes of the slice: x: 2, y: 2, z: 4, core: 2. Of those that a mesh axis runs over, the one named last changes fastest.
Arguments:
- voltages: bfloat16 [2, 512, 262144], P(None, 'stn', 'tm'), may hold values from -6 to 6
- delays: int32 [512], P('stn'), may hold values from 0 to 2048, as said below
- fringe: int32 [512], P('stn'), may hold values from 0 to 4095
- fringe_rate: int32 [512], P('stn'), may hold values from 0 to 4095
- filter_taps: float32 [16, 1024], replicated, may hold values from -1.5 to 1.5
Outputs:
- vis_real: float32 [1024, 512, 512], P(('stn', 'tm'))
- vis_imag: float32 [1024, 512, 512], P(('stn', 'tm'))
Inputs may be any that keep to these rules, and one draw needn't show every extreme that they name: `delays`: the largest delay over all stations is exactly 2048.
All inputs are finite; a program needn't handle non-finite values.
Results may differ from a plain program's by a relative error of at most 0.0066.
Values may be sent and summed in bfloat16 or wider, within the bound.
A program may use at most 448 MiB of HBM per device.

v0:
```python
import math

import jax
import jax.numpy as jnp
from jax import lax
from jax.sharding import PartitionSpec as P

C = 1024
P_SIZE = 16
Q = 4096
DMAX = 2048


TWO_PI = 2.0 * math.pi


def from_behind(block, axis, distance):
    devices = range(lax.axis_size(axis))
    route = [(i - distance, i) for i in devices if i - distance in devices]
    return lax.ppermute(block, axis, route)


def dft_tables(table_size):
    column = jnp.arange(table_size, dtype=jnp.int32)
    product = column[:, None] * column[None, :] % table_size
    angles = product.astype(jnp.float32) * (TWO_PI / table_size)
    return (jnp.cos(angles).astype(jnp.bfloat16), jnp.sin(angles).astype(jnp.bfloat16))


def channelize(delayed, filter_taps, fringe, fringe_rate, spectra, tables):
    stations = delayed.shape[1]
    blocks = delayed.reshape(2, stations, spectra + P_SIZE - 1, C)
    summed = jnp.zeros((2, stations, spectra, C), jnp.float32)
    for tap_index in range(P_SIZE):
        summed = summed + filter_taps[tap_index] * blocks[
            :, :, tap_index : tap_index + spectra
        ].astype(jnp.float32)
    weighted = summed.astype(jnp.bfloat16)
    weighted_rows = jnp.transpose(weighted, (1, 0, 2, 3)).reshape(stations, 2 * spectra, C)
    cosine_table, sine_table = tables
    with_cosine = jnp.einsum(
        "skn,nc->csk", weighted_rows, cosine_table, preferred_element_type=jnp.float32
    )
    with_sine = jnp.einsum(
        "skn,nc->csk", weighted_rows, sine_table, preferred_element_type=jnp.float32
    )
    inverse_root = 1.0 / math.sqrt(C)
    real_part = (with_cosine[..., :spectra] + with_sine[..., spectra:]) * inverse_root
    imag_part = (with_cosine[..., spectra:] - with_sine[..., :spectra]) * inverse_root
    channel = jnp.arange(C, dtype=jnp.int32)
    phase_index = (fringe[None, :] + fringe_rate[None, :] * channel[:, None]) % Q
    rotation = phase_index.astype(jnp.float32) * (TWO_PI / Q)
    rot_cos = jnp.cos(rotation)[:, :, None]
    rot_sin = jnp.sin(rotation)[:, :, None]
    out_real = real_part * rot_cos - imag_part * rot_sin
    out_imag = real_part * rot_sin + imag_part * rot_cos
    return jnp.concatenate([out_real, out_imag], axis=2).astype(jnp.bfloat16)


def products(left_rows, right_rows, swapped):
    gram_real = jnp.einsum(
        "cak,cbk->cab", left_rows, right_rows, preferred_element_type=jnp.float32
    )
    gram_imag = jnp.einsum("cak,cbk->cab", swapped, right_rows, preferred_element_type=jnp.float32)
    return (gram_real, gram_imag)


def local(voltages, delays, fringe, fringe_rate, filter_taps):
    samples = voltages.shape[2]
    spectra = samples // C
    stations = voltages.shape[1]
    early_rim = from_behind(voltages[:, :, samples - DMAX :], "tm", 1)
    late_rim = from_behind(voltages[:, :, : (P_SIZE - 1) * C], "tm", -1)
    extended = jnp.concatenate([early_rim, voltages, late_rim], axis=2)
    length = samples + (P_SIZE - 1) * C

    def select_window(station_row, delay_value):
        return lax.dynamic_slice_in_dim(station_row, DMAX - delay_value, length, 1)

    delayed = jax.vmap(select_window, in_axes=(1, 0), out_axes=1)(extended, delays)
    turned = channelize(delayed, filter_taps, fringe, fringe_rate, spectra, dft_tables(C))
    outgoing = turned.reshape(C, 1, stations, 2 * spectra)
    stn_count = lax.axis_size("stn")
    tm_count = lax.axis_size("tm")
    whole = stn_count * stations
    received = lax.all_to_all(outgoing, ("stn", "tm"), split_axis=0, concat_axis=1, tiled=True)
    grouped = received.reshape(-1, stn_count, tm_count, stations, 2, spectra)
    ordered = jnp.transpose(grouped, (0, 1, 3, 4, 2, 5))
    width = tm_count * spectra
    rows = ordered.reshape(-1, whole, 2 * width)
    swapped = jnp.concatenate([rows[..., width:], -rows[..., :width]], axis=-1)
    gram_real, gram_imag = products(rows, rows, swapped)
    inverse_count = 1.0 / (spectra * tm_count)
    return (gram_real * inverse_count, gram_imag * inverse_count)


def solution(mesh):
    return jax.shard_map(
        local,
        mesh=mesh,
        in_specs=(P(None, "stn", "tm"), P("stn"), P("stn"), P("stn"), P()),
        out_specs=(P(("stn", "tm"), None, None), P(("stn", "tm"), None, None)),
        check_vma=False,
    )
```

profile of v0, /device:TPU:0, one launch (start us, length us, event | category | flops | bytes accessed | tf_op | source)
XLA Modules:
  0.0 1555.2 jit_solution(17593143639046376881)
XLA Ops:
  0.7 30.9 %copy.24 = bf16[2,64,65536]{2,0,1:T(2,128)(2,1)} copy(bf16[2,64,65536]{2,1,0:T(8,128)(2,1)} %param.5) | data formatting | bytes 33554432 | tf_op args[0]
  31.6 6.7 slice.175
  47.3 52.9 %maximum_bitcast_fusion = bf16[64,2,82944]{2,1,0:T(2,128)(2,1)} fusion(bf16[2,64,15360]{2,0,1:T(2,128)(2,1)} %collective-permute-done.1, bf16[2,64,65536]{2,0,1:T(2,128)(2,1)} %copy.24, bf16[2,64,2048]{2,0,1:T(2,128)(2,1)S(1)} %collective-permute-done), kind=kLoop, calls=%fused_computation.4 | loop fusion | flops 63700992 | bytes 42467328 | tf_op jit(solution)/shard_map/vmap()/transpose | solution.py:78
  100.2 261.6 %while.1 = (s32[]{:T(128)}, bf16[64,2,82944]{2,1,0:T(2,128)(2,1)}, s32[64,3]{0,1:T(4,128)S(1)}, bf16[64,2,80896]{2,1,0:T(2,128)(2,1)}, s32[]{:T(128)}) while((s32[]{:T(128)}, bf16[64,2,82944]{2,1,0:T(2,128)(2,1)}, s32[64,3]{0,1:T(4,128)S(1)}, bf16[64,2,80896]{2,1,0:T(2,128)(2,1)}, s32[]{:T(128)}) %tuple.56), condition=%wide.while_cond, body=%wide.while_body.sunk | while | flops 2 | bytes 648809 | solution.py:78
  100.9 3.4 dynamic-slice_dynamic-update-slice_fusion.2
  105.0 3.4 dynamic-slice_dynamic-update-slice_fusion.2
  109.1 3.4 dynamic-slice_dynamic-update-slice_fusion.2
  113.2 3.4 dynamic-slice_dynamic-update-slice_fusion.2
  117.3 3.4 dynamic-slice_dynamic-update-slice_fusion.2
  121.4 3.4 dynamic-slice_dynamic-update-slice_fusion.2
  129.5 3.4 dynamic-slice_dynamic-update-slice_fusion.2
  133.6 3.4 dynamic-slice_dynamic-update-slice_fusion.2
  137.7 3.4 dynamic-slice_dynamic-update-slice_fusion.2
  141.8 3.4 dynamic-slice_dynamic-update-slice_fusion.2
  150.0 3.4 dynamic-slice_dynamic-update-slice_fusion.2
  158.1 3.4 dynamic-slice_dynamic-update-slice_fusion.2
  162.2 3.4 dynamic-slice_dynamic-update-slice_fusion.2
  166.3 3.4 dynamic-slice_dynamic-update-slice_fusion.2
  170.4 3.4 dynamic-slice_dynamic-update-slice_fusion.2
  178.6 3.4 dynamic-slice_dynamic-update-slice_fusion.2
  182.7 3.4 dynamic-slice_dynamic-update-slice_fusion.2
  186.7 3.4 dynamic-slice_dynamic-update-slice_fusion.2
  190.8 3.4 dynamic-slice_dynamic-update-slice_fusion.2
  194.9 3.4 dynamic-slice_dynamic-update-slice_fusion.2
  199.0 3.4 dynamic-slice_dynamic-update-slice_fusion.2
  207.2 3.4 dynamic-slice_dynamic-update-slice_fusion.2
  211.3 3.4 dynamic-slice_dynamic-update-slice_fusion.2
  215.4 3.4 dynamic-slice_dynamic-update-slice_fusion.2
  219.4 3.4 dynamic-slice_dynamic-update-slice_fusion.2
  227.6 3.4 dynamic-slice_dynamic-update-slice_fusion.2
  235.8 3.4 dynamic-slice_dynamic-update-slice_fusion.2
  239.9 3.4 dynamic-slice_dynamic-update-slice_fusion.2
  361.8 43.2 %reshape.162 = bf16[2,64,79,1024]{3,2,0,1:T(8,128)(2,1)} reshape(bf16[2,64,80896]{2,0,1:T(2,128)(2,1)} %bitcast.59) | data formatting | bytes 41418752 | tf_op jit(solution)/shard_map/reshape | solution.py:32
  405.1 216.3 %fusion.37 = (bf16[2,64,64,1024]{3,2,0,1:T(8,128)(2,1)}, bf16[2,64,64,1024]{3,2,0,1:T(8,128)(2,1)}, bf16[2,64,64,1024]{3,2,0,1:T(8,128)(2,1)}, bf16[2,64,64,1024...) fusion(bf16[2,64,79,1024]{3,2,0,1:T(8,128)(2,1)} %reshape.162), kind=kLoop, calls=%fused_computation.56 | loop fusion | bytes 536870912 | tf_op jit(solution)/shard_map/slice | solution.py:35
  621.6 93.5 %fusion.4 = bf16[64,2,64,1024]{3,2,0,1:T(8,128)(2,1)} fusion(bf16[2,64,64,1024]{3,2,0,1:T(8,128)(2,1)} %get-tuple-element.37, f32[1024]{0:T(1024)S(1)} %bitcast.76, bf16[2,64,64,1024]{3,2,0,1:T(8,128)(2,1)} %get-tuple-element.23, f32[1024]{0:T(1024)S(1)} %bitcast.77, bf16[2,64,64,1024]{3,2,0,1:T(8,128)(2,1)} %get-tuple-element.24, f32[1024]{0:T(1024)S(1)} %bitcast.63, ...), kind=kLoop, calls=%fused_computation.16 | loop fusion | flops 402653184 | bytes 285278208 | tf_op jit(solution)/shard_map/transpose | solution.py:39
  715.1 14.1 copy.28
  729.2 52.7 %fusion.16 = f32[1024,64,128]{0,2,1:T(8,128)} fusion(bf16[64,128,1024]{2,1,0:T(8,128)(2,1)} %bitcast.60), kind=kOutput, calls=%fused_computation.32 | convolution fusion | flops 17195597824 | bytes 50331648 | tf_op jit(solution)/shard_map/skn,nc->csk/dot_general | solution.py:41
  781.9 52.3 %fusion.19 = f32[1024,64,128]{0,2,1:T(8,128)} fusion(bf16[64,128,1024]{2,1,0:T(8,128)(2,1)} %bitcast.61), kind=kOutput, calls=%fused_computation.34 | convolution fusion | flops 17195597824 | bytes 50331648 | tf_op jit(solution)/shard_map/skn,nc->csk/dot_general | solution.py:44
  834.1 26.9 %fusion.7 = (bf16[1024,1,64,64]{0,3,2,1:T(8,128)(2,1)S(1)}, bf16[1024,1,64,64]{0,3,2,1:T(8,128)(2,1)}) fusion(f32[1024,64]{0,1:T(8,128)S(1)} %copy-done.1, f32[1024,64]{0,1:T(8,128)S(1)} %copy-done, f32[1024,64,128]{0,2,1:T(8,128)} %fusion.19, f32[1024,64,128]{0,2,1:T(8,128)} %fusion.16), kind=kLoop, calls=%fused_computation.17 | loop fusion | flops 41943040 | bytes 84410368 | tf_op jit(solution)/shard_map/concatenate | solution.py:57
  861.0 10.8 pad_maximum_fusion
  871.8 22.6 %copy.29 = bf16[1024,1,64,128]{3,2,1,0:T(8,128)(2,1)} copy(bf16[1024,1,64,128]{0,3,2,1:T(8,128)(2,1)} %pad_maximum_fusion) | data formatting | bytes 33554432 | tf_op jit(solution)/shard_map/concatenate | solution.py:57
  894.4 407.6 %all_to_all.15 = bf16[1024,1,64,128]{3,2,1,0:T(8,128)(2,1)} all-to-all(bf16[1024,1,64,128]{3,2,1,0:T(8,128)(2,1)} %copy.29), channel_id=1, replica_groups=mesh['stn'=8,'tm'=4] {'stn','tm'}, dimensions={0} | all-to-all | bytes 33554432 | tf_op jit(solution)/shard_map/all_to_all | solution.py:86
  1302.0 54.1 %reshape.135 = bf16[32,8,4,64,2,64]{5,4,3,0,2,1:T(2,128)(2,1)} reshape(bf16[32,32,1,64,128]{4,3,0,1,2:T(8,128)(2,1)} %bitcast.58) | data formatting | bytes 33554432 | tf_op jit(solution)/shard_map/reshape | solution.py:87
  1356.1 86.6 %copy.97 = bf16[32,8,4,64,2,64]{5,2,4,3,1,0:T(4,128)(2,1)} copy(bf16[32,8,4,64,2,64]{5,4,3,0,2,1:T(2,128)(2,1)} %reshape.135) | data formatting | bytes 33554432 | tf_op jit(solution)/shard_map/reshape | solution.py:87
  1442.7 51.4 %reshape.136 = bf16[32,512,512]{2,1,0:T(8,128)(2,1)} reshape(bf16[32,8,64,2,4,64]{5,4,3,2,1,0:T(4,128)(2,1)} %bitcast.57) | data formatting | bytes 33554432 | tf_op jit(solution)/shard_map/reshape | solution.py:90
  1494.1 11.3 fusion.38
  1505.4 25.9 %broadcast_multiply_fusion.1 = f32[32,512,512]{2,1,0:T(8,128)} fusion(bf16[32,512,512]{2,1,0:T(8,128)(2,1)} %reshape.136), kind=kOutput, calls=%fused_computation.13 | convolution fusion | flops 8598323200 | bytes 50331648 | tf_op jit(solution)/shard_map/cak,cbk->cab/dot_general | solution.py:61
  1531.3 23.6 %broadcast_multiply_fusion = f32[32,512,512]{2,1,0:T(8,128)} fusion(bf16[32,512,512]{2,1,0:T(8,128)(2,1)} %reshape.136, bf16[32,512,256]{2,1,0:T(8,128)(2,1)} %get-tuple-element.39, bf16[32,512,256]{2,1,0:T(8,128)(2,1)} %get-tuple-element.38), kind=kOutput, calls=%fused_computation.12 | convolution fusion | flops 8631877632 | bytes 67108864 | tf_op jit(solution)/shard_map/cak,cbk->cab/dot_general | solution.py:64
  (219 shorter events, 174.9 us)
Async XLA Ops:
  0.6 43.6 %copy-start.21 = (s32[64]{0:T(128)S(1)}, s32[64]{0:T(128)}, u32[]{:S(2)}) copy-start(s32[64]{0:T(128)} %param.6) | copy-start | bytes 772
  0.6 43.7 %copy-start.2 = (f32[16,1024]{1,0:T(8,128)S(1)}, f32[16,1024]{1,0:T(8,128)}, u32[]{:S(2)}) copy-start(f32[16,1024]{1,0:T(8,128)} %param.9) | copy-start | bytes 196612
  0.7 44.3 %copy-start.20 = (s32[64]{0:T(128)S(1)}, s32[64]{0:T(128)}, u32[]{:S(2)}) copy-start(s32[64]{0:T(128)} %param.7) | copy-start | bytes 772
  0.7 44.3 %copy-start.19 = (s32[64]{0:T(128)S(1)}, s32[64]{0:T(128)}, u32[]{:S(2)}) copy-start(s32[64]{0:T(128)} %param.8) | copy-start | bytes 772
  38.3 9.0 collective-permute-start.1
  41.0 6.0 collective-permute-start
  405.0 216.5 %copy-start.3 = (f32[1,1024]{1,0:T(1,128)S(1)}, f32[1,1024]{1,0:T(1,128)}, u32[]{:S(2)}) copy-start(f32[1,1024]{1,0:T(1,128)} %get-tuple-element.40) | copy-start | bytes 12292
  405.0 216.5 %copy-start.4 = (f32[1,1024]{1,0:T(1,128)S(1)}, f32[1,1024]{1,0:T(1,128)}, u32[]{:S(2)}) copy-start(f32[1,1024]{1,0:T(1,128)} %get-tuple-element.41) | copy-start | bytes 12292
  405.0 216.5 %copy-start.5 = (f32[1,1024]{1,0:T(1,128)S(1)}, f32[1,1024]{1,0:T(1,128)}, u32[]{:S(2)}) copy-start(f32[1,1024]{1,0:T(1,128)} %get-tuple-element.42) | copy-start | bytes 12292
  405.0 216.5 %copy-start.6 = (f32[1,1024]{1,0:T(1,128)S(1)}, f32[1,1024]{1,0:T(1,128)}, u32[]{:S(2)}) copy-start(f32[1,1024]{1,0:T(1,128)} %get-tuple-element.43) | copy-start | bytes 12292
  405.0 216.5 %copy-start.7 = (f32[1,1024]{1,0:T(1,128)S(1)}, f32[1,1024]{1,0:T(1,128)}, u32[]{:S(2)}) copy-start(f32[1,1024]{1,0:T(1,128)} %get-tuple-element.44) | copy-start | bytes 12292
  405.0 216.5 %copy-start.8 = (f32[1,1024]{1,0:T(1,128)S(1)}, f32[1,1024]{1,0:T(1,128)}, u32[]{:S(2)}) copy-start(f32[1,1024]{1,0:T(1,128)} %get-tuple-element.45) | copy-start | bytes 12292
  405.0 216.5 %copy-start.9 = (f32[1,1024]{1,0:T(1,128)S(1)}, f32[1,1024]{1,0:T(1,128)}, u32[]{:S(2)}) copy-start(f32[1,1024]{1,0:T(1,128)} %get-tuple-element.46) | copy-start | bytes 12292
  405.1 216.5 %copy-start.10 = (f32[1,1024]{1,0:T(1,128)S(1)}, f32[1,1024]{1,0:T(1,128)}, u32[]{:S(2)}) copy-start(f32[1,1024]{1,0:T(1,128)} %get-tuple-element.47) | copy-start | bytes 12292
  405.1 216.5 %copy-start.11 = (f32[1,1024]{1,0:T(1,128)S(1)}, f32[1,1024]{1,0:T(1,128)}, u32[]{:S(2)}) copy-start(f32[1,1024]{1,0:T(1,128)} %get-tuple-element.48) | copy-start | bytes 12292
  405.1 216.5 %copy-start.12 = (f32[1,1024]{1,0:T(1,128)S(1)}, f32[1,1024]{1,0:T(1,128)}, u32[]{:S(2)}) copy-start(f32[1,1024]{1,0:T(1,128)} %get-tuple-element.49) | copy-start | bytes 12292
  405.1 216.5 %copy-start.13 = (f32[1,1024]{1,0:T(1,128)S(1)}, f32[1,1024]{1,0:T(1,128)}, u32[]{:S(2)}) copy-start(f32[1,1024]{1,0:T(1,128)} %get-tuple-element.50) | copy-start | bytes 12292
  405.1 216.5 %copy-start.14 = (f32[1,1024]{1,0:T(1,128)S(1)}, f32[1,1024]{1,0:T(1,128)}, u32[]{:S(2)}) copy-start(f32[1,1024]{1,0:T(1,128)} %get-tuple-element.51) | copy-start | bytes 12292
  405.1 216.5 %copy-start.15 = (f32[1,1024]{1,0:T(1,128)S(1)}, f32[1,1024]{1,0:T(1,128)}, u32[]{:S(2)}) copy-start(f32[1,1024]{1,0:T(1,128)} %get-tuple-element.52) | copy-start | bytes 12292
  405.1 216.5 %copy-start.16 = (f32[1,1024]{1,0:T(1,128)S(1)}, f32[1,1024]{1,0:T(1,128)}, u32[]{:S(2)}) copy-start(f32[1,1024]{1,0:T(1,128)} %get-tuple-element.53) | copy-start | bytes 12292
  405.1 216.5 %copy-start.17 = (f32[1,1024]{1,0:T(1,128)S(1)}, f32[1,1024]{1,0:T(1,128)}, u32[]{:S(2)}) copy-start(f32[1,1024]{1,0:T(1,128)} %get-tuple-element.54) | copy-start | bytes 12292
  405.1 216.5 %copy-start.18 = (f32[1,1024]{1,0:T(1,128)S(1)}, f32[1,1024]{1,0:T(1,128)}, u32[]{:S(2)}) copy-start(f32[1,1024]{1,0:T(1,128)} %get-tuple-element.55) | copy-start | bytes 12292
  781.9 52.3 %copy-start = (f32[1024,64]{0,1:T(8,128)S(1)}, f32[1024,64]{0,1:T(8,128)}, u32[]{:S(2)}) copy-start(f32[1024,64]{0,1:T(8,128)} %get-tuple-element.56) | copy-start | bytes 786436
  781.9 52.3 %copy-start.1 = (f32[1024,64]{0,1:T(8,128)S(1)}, f32[1024,64]{0,1:T(8,128)}, u32[]{:S(2)}) copy-start(f32[1024,64]{0,1:T(8,128)} %get-tuple-element.57) | copy-start | bytes 786436
where the time goes:
time: 1570 us; the launch traced here: 1560 us
  local copies, waits for them, and re-layouts  790 us (50%)
  blocking collectives  408 us (26%)
  other arithmetic  197 us (13%)
  matrix products  154 us (10%)
    all_to_all x1, blocking collectives, local(): lax.all_to_all(outgoing, ('stn', 'tm'), split_axis=0, concat_axis=1, tile...  408 us
    gather x192, local copies, waits for them, and re-layouts  261 us
    slice x1, local copies, waits for them, and re-layouts, channelize(): blocks[:, :, tap_index:tap_index + spectra].astype(jnp.float32)  216 us
    reshape x2, local copies, waits for them, and re-layouts, local(): grouped = received.reshape(-1, stn_count, tm_count, stations, 2, spectra)  141 us
    transpose x1, other arithmetic, channelize(): jnp.transpose(weighted, (1, 0, 2, 3)).reshape(stations, 2 * spectra, C)  93.5 us
    transpose x1, other arithmetic, select_window(): return lax.dynamic_slice_in_dim(station_row, DMAX - delay_value, length, 1)  52.9 us
    dot_general x1, matrix products, channelize(): jnp.einsum('skn,nc->csk', weighted_rows, cosine_table, preferred_element_...  52.7 us
    dot_general x1, matrix products, channelize(): jnp.einsum('skn,nc->csk', weighted_rows, sine_table, preferred_element_ty...  52.3 us
  transfers between devices with their start and end apart: 2, of which 1 were waited for; matrix products, arithmetic and copies ran while one was open for 0% of the time, Pallas kernels for 0%

commit v1 on v0

v1 whole, which is shorter than its diff:
```python
import functools
import math

import jax
import jax.numpy as jnp
from jax import lax
from jax.experimental import pallas as pl
from jax.experimental.pallas import tpu as pltpu
from jax.sharding import PartitionSpec as P

C = 1024
P_SIZE = 16
Q = 4096
DMAX = 2048


TWO_PI = 2.0 * math.pi


def from_behind(block, axis, distance):
    devices = range(lax.axis_size(axis))
    route = [(i - distance, i) for i in devices if i - distance in devices]
    return lax.ppermute(block, axis, route)


def dft_tables(table_size):
    column = jnp.arange(table_size, dtype=jnp.int32)
    product = column[:, None] * column[None, :] % table_size
    angles = product.astype(jnp.float32) * (TWO_PI / table_size)
    return (jnp.cos(angles).astype(jnp.bfloat16), jnp.sin(angles).astype(jnp.bfloat16))


def window_filter_kernel(delay_ref, taps_ref, early_ref, main_ref, late_ref, out_ref, rolled, shifted):
    early_rows, spectra, late_rows = early_ref.shape[2], main_ref.shape[2], late_ref.shape[2]
    need = -(-(spectra + P_SIZE - 1) // 8) * 8
    start = early_rows * C - delay_ref[pl.program_id(0)]
    skip = start // C
    within = start % C
    amount = (C - within) % C
    lane = lax.broadcasted_iota(jnp.int32, (8, C), 1)
    ahead = skip + jnp.where(lane < C - within, 0, 1)
    for part in range(2):
        first = pltpu.roll(early_ref[part, 0].astype(jnp.float32), amount, 1)
        rolled[0:early_rows, :] = first[0:early_rows]
        for row in range(0, spectra, 8):
            rolled[early_rows + row : early_rows + row + 8, :] = pltpu.roll(
                main_ref[part, 0, row : row + 8, :].astype(jnp.float32), amount, 1
            )
        base = early_rows + spectra
        for row in range(0, late_rows, 8):
            rolled[base + row : base + row + 8, :] = pltpu.roll(
                late_ref[part, 0, row : row + 8, :].astype(jnp.float32), amount, 1
            )
        for row in range(0, need, 8):
            chosen = rolled[row : row + 8, :]
            for step in range(1, early_rows + 2):
                chosen = jnp.where(ahead == step, rolled[row + step : row + step + 8, :], chosen)
            shifted[row : row + 8, :] = chosen
        for left in range(0, C, 256):
            for row in range(0, spectra, 16):
                total = jnp.zeros((16, 256), jnp.float32)
                for tap in range(P_SIZE):
                    total = total + taps_ref[tap : tap + 1, left : left + 256] * shifted[
                        row + tap : row + tap + 16, left : left + 256
                    ]
                out_ref[0, part, row : row + 16, left : left + 256] = total.astype(jnp.bfloat16)


def window_filter(delays, filter_taps, early, main, late):
    stations, spectra = main.shape[1], main.shape[2]
    early_rows, late_rows = early.shape[2], late.shape[2]
    need = -(-(spectra + P_SIZE - 1) // 8) * 8
    rows = need + early_rows + 8

    def block(count):
        return pl.BlockSpec((2, 1, count, C), lambda s: (0, s, 0, 0))

    return pl.pallas_call(
        window_filter_kernel,
        grid=(stations,),
        in_specs=[
            pl.BlockSpec(memory_space=pltpu.SMEM),
            pl.BlockSpec((P_SIZE, C), lambda s: (0, 0)),
            block(early_rows),
            block(spectra),
            block(late_rows),
        ],
        out_specs=pl.BlockSpec((1, 2, spectra, C), lambda s: (s, 0, 0, 0)),
        out_shape=jax.ShapeDtypeStruct((stations, 2, spectra, C), jnp.bfloat16),
        scratch_shapes=[pltpu.VMEM((rows, C), jnp.float32), pltpu.VMEM((need, C), jnp.float32)],
    )(delays, filter_taps, early, main, late)


def channelize(weighted_rows, fringe, fringe_rate, spectra, tables):
    cosine_table, sine_table = tables
    with_cosine = jnp.einsum(
        "skn,nc->csk", weighted_rows, cosine_table, preferred_element_type=jnp.float32
    )
    with_sine = jnp.einsum(
        "skn,nc->csk", weighted_rows, sine_table, preferred_element_type=jnp.float32
    )
    inverse_root = 1.0 / math.sqrt(C)
    real_part = (with_cosine[..., :spectra] + with_sine[..., spectra:]) * inverse_root
    imag_part = (with_cosine[..., spectra:] - with_sine[..., :spectra]) * inverse_root
    channel = jnp.arange(C, dtype=jnp.int32)
    phase_index = (fringe[None, :] + fringe_rate[None, :] * channel[:, None]) % Q
    rotation = phase_index.astype(jnp.float32) * (TWO_PI / Q)
    rot_cos = jnp.cos(rotation)[:, :, None]
    rot_sin = jnp.sin(rotation)[:, :, None]
    out_real = real_part * rot_cos - imag_part * rot_sin
    out_imag = real_part * rot_sin + imag_part * rot_cos
    return jnp.concatenate([out_real, out_imag], axis=2).astype(jnp.bfloat16)


def gram_kernel(scale, spectra_ref, real_ref, imag_ref):
    stn_count, tm_count, stations, width = spectra_ref.shape[1:]
    lane = lax.broadcasted_iota(jnp.int32, (stn_count * stations, width), 1)
    pieces, turned_pieces = [], []
    for source in range(tm_count):
        piece = spectra_ref[0, :, source].reshape(stn_count * stations, width)
        turned = pltpu.roll(piece.astype(jnp.float32), width // 2, 1)
        pieces.append(piece)
        turned_pieces.append(jnp.where(lane < width // 2, turned, -turned).astype(jnp.bfloat16))
    rows = jnp.concatenate(pieces, axis=1)
    swapped = jnp.concatenate(turned_pieces, axis=1)
    last = (((1,), (1,)), ((), ()))
    real_ref[0] = lax.dot_general(rows, rows, last, preferred_element_type=jnp.float32) * scale
    imag_ref[0] = lax.dot_general(swapped, rows, last, preferred_element_type=jnp.float32) * scale


def grams(grouped, scale):
    channels, stn_count, tm_count, stations, width = grouped.shape
    whole = stn_count * stations
    result = jax.ShapeDtypeStruct((channels, whole, whole), jnp.float32)
    return pl.pallas_call(
        functools.partial(gram_kernel, scale),
        grid=(channels,),
        in_specs=[pl.BlockSpec((1, *grouped.shape[1:]), lambda c: (c, 0, 0, 0, 0))],
        out_specs=[pl.BlockSpec((1, whole, whole), lambda c: (c, 0, 0))] * 2,
        out_shape=[result, result],
    )(grouped)


def local(voltages, delays, fringe, fringe_rate, filter_taps):
    samples = voltages.shape[2]
    spectra = samples // C
    stations = voltages.shape[1]
    frames = voltages.reshape(2, stations, spectra, C)
    early = from_behind(frames[:, :, spectra - DMAX // C :], "tm", 1)
    late = from_behind(frames[:, :, :P_SIZE], "tm", -1)
    weighted = window_filter(delays, filter_taps, early, frames, late)
    weighted_rows = weighted.reshape(stations, 2 * spectra, C)
    turned = channelize(weighted_rows, fringe, fringe_rate, spectra, dft_tables(C))
    outgoing = turned.reshape(C, 1, stations, 2 * spectra)
    stn_count = lax.axis_size("stn")
    tm_count = lax.axis_size("tm")
    received = lax.all_to_all(outgoing, ("stn", "tm"), split_axis=0, concat_axis=1, tiled=True)
    grouped = received.reshape(-1, stn_count, tm_count, stations, 2 * spectra)
    real, imag = grams(grouped, 1.0 / (spectra * tm_count))
    return (real, imag)


def solution(mesh):
    return jax.shard_map(
        local,
        mesh=mesh,
        in_specs=(P(None, "stn", "tm"), P("stn"), P("stn"), P("stn"), P()),
        out_specs=(P(("stn", "tm"), None, None), P(("stn", "tm"), None, None)),
        check_vma=False,
    )
```

time: 1570 us -> 776 us (0.49)
  local copies, waits for them, and re-layouts: 790 us -> 51.1 us
  Pallas kernels: 0 us -> 167 us
  other arithmetic: 197 us -> 38.6 us
  matrix products: 154 us -> 104 us
    gather x192 -> x0, local copies, waits for them, and re-layouts: 261 us -> none
    reshape x4 -> x0, local copies, waits for them, and re-layouts: 235 us -> none  [the longest x2 141 us: local(): grouped = received.reshape(-1, stn_count, tm_count, stations, 2, spectra)]
    slice x4 -> x2, local copies, waits for them, and re-layouts: 225 us -> 1.39 us  [the longest x1 0.83 us: local(): late = from_behind(frames[:, :, :P_SIZE], 'tm', -1)]
    pallas_call x0 -> x2, Pallas kernels: none -> 167 us  [the longest x1 130 us: window_filter(): pl.pallas_call(window_filter_kernel, grid=(stations,), in_specs=[pl.Block...]
    transpose x2 -> x0, other arithmetic: 146 us -> none  [the longest x1 93.5 us: channelize(): jnp.transpose(weighted, (1, 0, 2, 3)).reshape(stations, 2 * spectra, C)]
    dot_general x2 -> x0, matrix products: 49.5 us -> none  [the longest x1 25.9 us: products(): jnp.einsum('cak,cbk->cab', left_rows, right_rows, preferred_element_type=...]
where the time goes in v1:
time: 776 us; the launch traced here: 775 us
  blocking collectives  409 us (53%)
  Pallas kernels  167 us (22%)
  matrix products  104 us (13%)
  local copies, waits for them, and re-layouts  51.1 us (7%)
  other arithmetic  38.6 us (5%)
    all_to_all x1, blocking collectives, local(): lax.all_to_all(outgoing, ('stn', 'tm'), split_axis=0, concat_axis=1, tile...  409 us
    pallas_call x1, Pallas kernels, window_filter(): pl.pallas_call(window_filter_kernel, grid=(stations,), in_specs=[pl.Block...  130 us
    dot_general x1, matrix products, channelize(): jnp.einsum('skn,nc->csk', weighted_rows, cosine_table, preferred_element_...  52.3 us
    dot_general x1, matrix products, channelize(): jnp.einsum('skn,nc->csk', weighted_rows, sine_table, preferred_element_ty...  52.2 us
    concatenate x2, other arithmetic, channelize(): return jnp.concatenate([out_real, out_imag], axis=2).astype(jnp.bfloat16)  37.5 us
    pallas_call x1, Pallas kernels, grams(): pl.pallas_call(functools.partial(gram_kernel, scale), grid=(channels,), i...  36.9 us
    concatenate x1, local copies, waits for them, and re-layouts, channelize(): return jnp.concatenate([out_real, out_imag], axis=2).astype(jnp.bfloat16)  22.6 us
    unnamed x9, local copies, waits for them, and re-layouts  20.4 us
  transfers between devices with their start and end apart: 2, of which 1 were waited for; matrix products, arithmetic and copies ran while one was open for 0% of the time, Pallas kernels for 0%

profile of v1, /device:TPU:0, one launch (start us, length us, event | category | flops | bytes accessed | tf_op | source)
XLA Modules:
  0.0 774.5 jit_solution(4921019722438588720)
XLA Ops:
  0.6 15.6 %copy.12 = bf16[16,8,64,1024]{3,2,1,0:T(8,128)(2,1)S(1)} copy(bf16[16,8,64,1024]{3,1,2,0:T(8,128)(2,1)} %bitcast.28) | data formatting | bytes 33554432
  16.3 0.0 copy-start
  16.3 0.0 copy-start.2
  16.3 0.0 copy-start.3
  16.3 0.8 slice.25
  17.1 1.3 collective-permute-start.1
  18.4 4.0 copy-done
  22.4 0.6 slice.24
  23.0 2.6 collective-permute-start
  25.6 0.0 copy-done.2
  25.6 0.0 copy-done.3
  25.6 1.1 cosine_multiply_fusion
  26.8 0.2 collective-permute-done.early_ref
  26.9 0.0 copy-start.1
  26.9 0.0 collective-permute-done.1.late_ref
  26.9 0.8 copy-done.1
  27.7 130.2 %shard_map.68 = bf16[64,2,64,1024]{3,2,1,0:T(8,128)(2,1)} custom-call(s32[64]{0:T(128)} %delay_ref.1, f32[16,1024]{1,0:T(8,128)} %taps_ref.1, bf16[2,64,2,1024]{3,2,1,0:T(2,128)(2,1)} %copy-done.1, bf16[2,64,64,1024]{3,2,1,0:T(8,128)(2,1)} %bitcast.23, bf16[2,64,16,1024]{3,2,1,0:T(8,128)(2,1)} %collective-permute-done.1.late_ref), custom_call_target="tpu_custom_call" | custom-call | tf_op jit(solution)/shard_map/pallas_call | solution.py:78
  157.9 52.2 %fusion.12 = f32[1024,64,128]{0,2,1:T(8,128)} fusion(bf16[64,128,1024]{2,1,0:T(8,128)(2,1)} %bitcast.26), kind=kOutput, calls=%fused_computation.21 | convolution fusion | flops 17195597824 | bytes 50331648 | tf_op jit(solution)/shard_map/skn,nc->csk/dot_general | solution.py:99
  210.1 52.3 %fusion.9 = f32[1024,64,128]{0,2,1:T(8,128)} fusion(bf16[64,128,1024]{2,1,0:T(8,128)(2,1)} %bitcast.27), kind=kOutput, calls=%fused_computation.19 | convolution fusion | flops 17195597824 | bytes 50331648 | tf_op jit(solution)/shard_map/skn,nc->csk/dot_general | solution.py:96
  262.4 26.6 %fusion = (bf16[1024,1,64,64]{0,3,2,1:T(8,128)(2,1)S(1)}, bf16[1024,1,64,64]{0,3,2,1:T(8,128)(2,1)}) fusion(f32[1024,64]{0,1:T(8,128)S(1)} %get-tuple-element.5, f32[1024,64]{0,1:T(8,128)S(1)} %get-tuple-element.4, f32[1024,64,128]{0,2,1:T(8,128)} %fusion.12, f32[1024,64,128]{0,2,1:T(8,128)} %fusion.9), kind=kLoop, calls=%fused_computation.5 | loop fusion | flops 41943040 | bytes 84410368 | tf_op jit(solution)/shard_map/concatenate | solution.py:112
  289.0 10.8 %pad_maximum_fusion = bf16[1024,1,64,128]{0,3,2,1:T(8,128)(2,1)} fusion(bf16[1024,1,64,64]{0,3,2,1:T(8,128)(2,1)} %get-tuple-element.3, bf16[1024,1,64,64]{0,3,2,1:T(8,128)(2,1)S(1)} %get-tuple-element.2), kind=kLoop, calls=%fused_computation.2 | loop fusion | flops 33554432 | bytes 33554432 | tf_op jit(solution)/shard_map/concatenate | solution.py:112
  299.8 22.6 %copy.10 = bf16[1024,1,64,128]{3,2,1,0:T(8,128)(2,1)} copy(bf16[1024,1,64,128]{0,3,2,1:T(8,128)(2,1)} %pad_maximum_fusion) | data formatting | bytes 33554432 | tf_op jit(solution)/shard_map/concatenate | solution.py:112
  322.4 408.5 %all_to_all.15 = bf16[1024,1,64,128]{3,2,1,0:T(8,128)(2,1)S(1)} all-to-all(bf16[1024,1,64,128]{3,2,1,0:T(8,128)(2,1)} %copy.10), channel_id=1, replica_groups=mesh['stn'=8,'tm'=4] {'stn','tm'}, dimensions={0} | all-to-all | bytes 33554432 | tf_op jit(solution)/shard_map/all_to_all | solution.py:157
  730.9 6.7 copy.11
  737.6 36.9 %shard_map.69 = (f32[32,512,512]{2,1,0:T(8,128)}, f32[32,512,512]{2,1,0:T(8,128)}) custom-call(bf16[32,8,4,64,128]{4,3,2,1,0:T(8,128)(2,1)} %bitcast.24), custom_call_target="tpu_custom_call" | custom-call | tf_op jit(solution)/shard_map/pallas_call | solution.py:135
Async XLA Ops:
  16.3 6.2 copy-start
  16.3 9.3 %copy-start.2 = (s32[64]{0:T(128)S(1)}, s32[64]{0:T(128)}, u32[]{:S(2)}) copy-start(s32[64]{0:T(128)} %param.8) | copy-start | bytes 772
  16.3 9.3 %copy-start.3 = (s32[64]{0:T(128)S(1)}, s32[64]{0:T(128)}, u32[]{:S(2)}) copy-start(s32[64]{0:T(128)} %param.7) | copy-start | bytes 772
  17.1 9.8 %collective-permute-start.1 = (bf16[2,64,16,1024]{3,2,1,0:T(8,128)(2,1)S(1)}, bf16[2,64,16,1024]{3,2,1,0:T(8,128)(2,1)}, u32[]{:S(2)}, u32[]{:S(2)}) collective-permute-start(bf16[2,64,16,1024]{3,2,1,0:T(8,128)(2,1)S(1)} %slice.25), channel_id=1, source_target_pairs={{1,0},{2,1},{3,2},{5,4},{6,5},{7,6},{9,8},{10,9},{11,10},{13,12},{... | collective-permute-start | bytes 12582920 | tf_op jit(solution)/shard_map/ppermute | solution.py:23
  23.0 3.9 collective-permute-start
  26.9 0.8 copy-start.1
